TPU v7x, 32 devices: a whole 2x2x4 slice. The times are simulated.
32 devices in a mesh: groups: 2 (over x), band: 8 (over z, y), sub: 2 (over core).
Axes of the slice: x: 2, y: 2, z: 4, core: 2. Of those that a mesh axis runs over, the one named last changes fastest.
Arguments:
- sky_maps: bfloat16 [32, 2, 32, 16384], P(('groups', 'band', 'sub')), parts along dimension 0, may hold values from -6 to 6
- sky_mask: float32 [32, 16384], P(('groups', 'band', 'sub')), parts along dimension 0, may hold values from 0.005 to 1, as said below
- pixel_counts: int32 [32], P(('groups', 'band', 'sub')), parts along dimension 0, may hold values from 8192 to 16384, as said below
- phi_offsets: int32 [32], P(('groups', 'band', 'sub')), parts along dimension 0, may hold values from 0 to 1
- low_orders: int32 [32], P('groups'), parts along dimension 0, may hold values from 1 to 4095, as said below
- legendre: bfloat16 [32, 8192, 32], P(('groups', 'band', 'sub')), parts along dimension 0, may hold values from -1 to 1
Outputs:
- alm_packed: float32 [32, 8192, 128], P(('groups', 'band', 'sub')), parts along dimension 0
- spectra: float32 [16384, 2, 1024], P(('groups', 'band', 'sub')), parts along dimension 0
There are 2 independent parts, one for each index of `groups`. A program takes and returns all parts, laid end to end along the dimension named above; each array names one. Nothing has to cross between parts.
Inputs may be any that keep to these rules, and one draw needn't show every extreme that they name: `pixel_counts`: multiples of 4; some cycle has exactly 16384 pixels; pixel slots at or past a cycle's count are not used. `low_orders`: all distinct. `sky_mask`: Positive.
All inputs are finite; a program needn't handle non-finite values.
Results may differ from a plain program's by a relative error of at most 0.0046.
Values may be sent and summed in bfloat16 or wider, within the bound.
A program may use at most 128 MiB of HBM per device.

v0:
```python
import jax
import jax.numpy as jnp
from jax import lax
from jax.sharding import PartitionSpec as P


def slot_orders(low_orders, degree_count):
    return jnp.stack([low_orders, degree_count - low_orders], axis=1).reshape(-1)


def finish_cycle(pixel_sums, cycle_count, orders):
    slots = orders.shape[0]
    maps_count = pixel_sums.shape[1] // 2
    inverse_root = 1.0 / jnp.sqrt(cycle_count.astype(jnp.float32))
    real_part = (pixel_sums[:slots] * inverse_root).reshape(slots, 2, maps_count)
    imag_part = (-pixel_sums[slots:] * inverse_root).reshape(slots, 2, maps_count)
    joined = jnp.stack(
        [real_part[:, 0], imag_part[:, 0], real_part[:, 1], imag_part[:, 1]], axis=1
    ).reshape(slots, 4 * maps_count)
    live_slots = 2 * orders < cycle_count
    return jnp.where(live_slots[:, None], joined, 0.0).astype(jnp.bfloat16)


def cycle_fourier(cycle_maps, cycle_mask, cycle_count, cycle_offset, orders):
    maps_count = cycle_maps.shape[1]
    pixel_slots = cycle_maps.shape[2]
    cycle_rows = cycle_maps.reshape(2 * maps_count, pixel_slots)
    block_width = min(2048, pixel_slots)
    group_count = block_width // 128
    slots = orders.shape[0]
    modulus = 2 * cycle_count
    scale = jnp.pi / cycle_count.astype(jnp.float32)
    order_mod = orders % modulus
    fine_units = 2 * order_mod[:, None] * jnp.arange(128, dtype=jnp.int32)[None, :] % modulus
    fine_angle = scale * fine_units.astype(jnp.float32)
    fine_cos = jnp.cos(fine_angle)[:, None, :]
    fine_sin = jnp.sin(fine_angle)[:, None, :]

    def add_block(block_index, totals):
        first_pixel = block_index * block_width
        row_block = lax.dynamic_slice_in_dim(cycle_rows, first_pixel, block_width, 1)
        mask_block = lax.dynamic_slice_in_dim(cycle_mask, first_pixel, block_width, 0)
        pixels = first_pixel + jnp.arange(block_width, dtype=jnp.int32)
        masked = jnp.where(
            pixels[None, :] < cycle_count, mask_block[None, :] * row_block.astype(jnp.float32), 0.0
        ).astype(jnp.bfloat16)
        group_starts = first_pixel + 128 * jnp.arange(group_count, dtype=jnp.int32)
        coarse_units = (
            order_mod[:, None] * ((2 * group_starts[None, :] + cycle_offset) % modulus) % modulus
        )
        coarse_angle = scale * coarse_units.astype(jnp.float32)
        coarse_cos = jnp.cos(coarse_angle)[:, :, None]
        coarse_sin = jnp.sin(coarse_angle)[:, :, None]
        cosines = (coarse_cos * fine_cos - coarse_sin * fine_sin).reshape(slots, block_width)
        sines = (coarse_sin * fine_cos + coarse_cos * fine_sin).reshape(slots, block_width)
        tables = jnp.concatenate([cosines.astype(jnp.bfloat16), sines.astype(jnp.bfloat16)], axis=0)
        return totals + lax.dot_general(
            tables, masked, (((1,), (1,)), ((), ())), preferred_element_type=jnp.float32
        )

    block_count = (cycle_count + block_width - 1) // block_width
    pixel_sums = lax.fori_loop(
        0, block_count, add_block, jnp.zeros((2 * slots, 2 * maps_count), jnp.float32)
    )
    return finish_cycle(pixel_sums, cycle_count, orders)


def stacked_operand(block_rows):
    quarter = block_rows.shape[1] // 4
    q_real = block_rows[:, :quarter]
    q_imag = block_rows[:, quarter : 2 * quarter]
    u_real = block_rows[:, 2 * quarter : 3 * quarter]
    u_imag = block_rows[:, 3 * quarter :]
    lower_half = jnp.concatenate([u_imag, -u_real, -q_imag, q_real], axis=1)
    return jnp.concatenate([block_rows, lower_half], axis=0)


def pair_alm(legendre_rows, first_order, first_block, second_block):
    first_operand = stacked_operand(first_block)
    second_operand = stacked_operand(second_block)
    degree_count, inner_width = legendre_rows.shape
    tile_height = min(128, degree_count)
    tile_count = degree_count // tile_height
    split_row = degree_count - first_order
    tile_starts = jnp.arange(tile_count, dtype=jnp.int32) * tile_height
    chosen = jnp.where(
        (tile_starts < split_row)[:, None, None], first_operand[None], second_operand[None]
    )
    tile_product = jnp.einsum(
        "tir,tro->tio",
        legendre_rows.reshape(tile_count, tile_height, inner_width),
        chosen,
        preferred_element_type=jnp.float32,
    )
    tile_product = tile_product.reshape(degree_count, first_operand.shape[1])
    border = split_row // tile_height * tile_height
    border_rows = lax.dynamic_slice_in_dim(legendre_rows, border, tile_height, 0)
    border_product = jnp.dot(border_rows, second_operand, preferred_element_type=jnp.float32)
    current = lax.dynamic_slice_in_dim(tile_product, border, tile_height, 0)
    row_index = border + jnp.arange(tile_height, dtype=jnp.int32)
    patched = jnp.where((row_index >= split_row)[:, None], border_product, current)
    return -lax.dynamic_update_slice_in_dim(tile_product, patched, border, 0)


def dense_pair(alm_rows, first_order):
    degree_count = alm_rows.shape[0]
    degrees = jnp.arange(degree_count, dtype=jnp.int32)
    first_dense = jnp.where(
        (degrees >= first_order)[:, None], jnp.roll(alm_rows, first_order, axis=0), 0.0
    ).astype(jnp.bfloat16)
    second_dense = jnp.where(
        (degrees >= degree_count - first_order)[:, None], alm_rows, 0.0
    ).astype(jnp.bfloat16)
    return jnp.stack([first_dense, second_dense], axis=0)


def outer_totals(rows, maps_count):
    split_parts = rows.reshape(rows.shape[0], rows.shape[1], 2, 2, maps_count)
    return jnp.einsum(
        "slerm,slern->lemn", split_parts, split_parts, preferred_element_type=jnp.float32
    )


def scaled_spectra(totals, degrees, orders, weight, maps_count):
    counts = jnp.maximum(
        jnp.sum((orders[None, :] <= degrees[:, None]).astype(jnp.int32), axis=1), 1
    ).astype(jnp.float32)
    return (2.0 * totals / (weight * counts)[:, None, None, None]).reshape(
        degrees.shape[0], 2, maps_count * maps_count
    )


def local(sky_maps, sky_mask, pixel_counts, phi_offsets, low_orders, legendre):
    devices = lax.axis_size(("band", "sub"))
    device_index = lax.axis_index(("band", "sub"))
    degree_count = legendre.shape[1]
    orders = slot_orders(low_orders, degree_count)
    cycle_local = sky_maps.shape[0]
    maps_count = sky_maps.shape[2]
    pair_local = legendre.shape[0]
    slot_local = 2 * pair_local
    columns = 4 * maps_count
    valid_pixels = jnp.arange(sky_maps.shape[3], dtype=jnp.int32)[None, :] < pixel_counts[:, None]
    local_square = jnp.sum(jnp.where(valid_pixels, sky_mask * sky_mask, 0.0))
    local_pixels = jnp.sum(pixel_counts.astype(jnp.float32))
    total_square, total_pixels = lax.psum((local_square, local_pixels), ("band", "sub"))
    weight = total_square / total_pixels
    cycle_blocks = [
        cycle_fourier(sky_maps[0], sky_mask[0], pixel_counts[0], phi_offsets[0], orders)
    ]
    coefficients = jnp.stack(cycle_blocks, axis=1).reshape(
        devices, slot_local, cycle_local, columns
    )
    received = lax.all_to_all(
        coefficients, ("band", "sub"), split_axis=0, concat_axis=0, tiled=True
    )
    cycle_total = devices * cycle_local
    first_order = lax.dynamic_index_in_dim(
        low_orders, device_index * pair_local + 0, 0, keepdims=False
    )
    first_block = received[:, 0].reshape(cycle_total, columns)
    second_block = received[:, 1].reshape(cycle_total, columns)
    alm_pairs = [pair_alm(legendre[0], first_order, first_block, second_block)]
    alm_packed = jnp.stack(alm_pairs, axis=0)
    dense_local = dense_pair(alm_pairs[0], first_order)
    by_degree = lax.all_to_all(
        dense_local, ("band", "sub"), split_axis=1, concat_axis=0, tiled=True
    )
    degree_local = by_degree.shape[1]
    degrees = device_index * degree_local + jnp.arange(degree_local, dtype=jnp.int32)
    totals = outer_totals(by_degree, maps_count)
    spectra = scaled_spectra(totals, degrees, orders, weight, maps_count)
    return (alm_packed, spectra)


def solution(mesh):
    placed = (
        P(("groups", "band", "sub"), None, None, None),
        P(("groups", "band", "sub"), None),
        P(("groups", "band", "sub")),
        P(("groups", "band", "sub")),
        P("groups"),
        P(("groups", "band", "sub"), None, None),
    )
    return jax.shard_map(
        local,
        mesh=mesh,
        in_specs=placed,
        out_specs=(
            P(("groups", "band", "sub"), None, None),
            P(("groups", "band", "sub"), None, None),
        ),
        check_vma=False,
    )
```

profile of v0, /device:TPU:18, one launch (start us, length us, event | category | flops | bytes accessed | tf_op | source)
XLA Modules:
  0.0 302.1 jit_solution(14685588854479680032)
XLA Ops:
  1.4 0.7 subtract_bitcast_fusion
  2.0 0.7 pad_add_fusion
  3.1 34.6 %while.14 = (s32[]{:T(128)}, f32[64,64]{1,0:T(8,128)S(1)}, s32[]{:T(128)}, f32[]{:T(128)}, s32[32]{0:T(128)S(1)}, /*index=5*/s32[]{:T(128)}, s32[]{:T(128)}, pre...) while((s32[]{:T(128)}, f32[64,64]{1,0:T(8,128)S(1)}, ...), condition=%wide.region_1.2_spmd.clone.clone, body=%wide.region_0.1_spmd.clone.clone.sunk | while | flops 18404532 | bytes 1446522 | solution.py:62
  3.4 0.8 and_select_fusion.4
  4.2 0.4 fusion.55
  4.8 0.7 dynamic_slice.63
  5.5 0.7 add_compare_fusion.3
  6.2 1.2 convolution_add_fusion.2
  7.4 0.4 cosine_bitcast_fusion.2
  7.8 0.8 and_select_fusion.4
  8.5 0.4 fusion.55
  9.2 0.7 dynamic_slice.63
  9.9 0.7 add_compare_fusion.3
  10.5 1.2 convolution_add_fusion.2
  12.1 0.8 and_select_fusion.4
  12.9 0.4 fusion.55
  13.5 0.7 dynamic_slice.63
  14.2 0.7 add_compare_fusion.3
  14.9 1.2 convolution_add_fusion.2
  16.4 0.8 and_select_fusion.4
  17.2 0.4 fusion.55
  17.8 0.7 dynamic_slice.63
  18.5 0.7 add_compare_fusion.3
  19.2 1.2 convolution_add_fusion.2
  20.4 0.4 cosine_bitcast_fusion.2
  20.8 0.8 and_select_fusion.4
  21.5 0.4 fusion.55
  22.2 0.7 dynamic_slice.63
  22.9 0.7 add_compare_fusion.3
  23.5 1.2 convolution_add_fusion.2
  24.7 0.4 cosine_bitcast_fusion.2
  25.1 0.8 and_select_fusion.4
  25.9 0.4 fusion.55
  26.5 0.7 dynamic_slice.63
  27.2 0.7 add_compare_fusion.3
  27.9 1.2 convolution_add_fusion.2
  29.1 0.4 cosine_bitcast_fusion.2
  29.4 0.8 and_select_fusion.4
  30.8 0.7 dynamic_slice.63
  31.5 0.7 add_compare_fusion.3
  32.2 1.2 convolution_add_fusion.2
  33.7 0.8 and_select_fusion.4
  35.2 0.7 dynamic_slice.63
  35.9 0.7 add_compare_fusion.3
  36.5 1.2 convolution_add_fusion.2
  38.3 0.7 select_convert_fusion.3
  38.9 5.6 %all-to-all-start = ((bf16[16,2,1,128]{3,1,2,0:T(2,128)(2,1)}), bf16[16,2,1,128]{3,1,2,0:T(2,128)(2,1)S(1)}, u32[]{:S(2)}, u32[]{:S(2)}) async-start(bf16[16,2,1,128]{3,1,2,0:T(2,128)(2,1)} %select_convert_fusion.3), calls=%async_computation | async-start | bytes 16384 | tf_op jit(solution)/shard_map/all_to_all | solution.py:154
  44.6 0.6 dynamic_slice.26
  45.8 0.7 iota_compare_fusion.1
  49.0 0.9 fusion.34
  50.3 5.4 %fusion.31 = (bf16[1,8192,128]{2,1,0:T(8,128)(2,1)S(1)}, f32[1,8192,128]{2,1,0:T(8,128)}) fusion(pred[8192]{0:T(1024)(128)(4,1)S(1)} %iota_compare_fusion, f32[8192,128]{1,0:T(8,128)S(1)} %fusion.33), kind=kLoop, calls=%fused_computation.49 | loop fusion | flops 3145728 | bytes 10493952 | tf_op jit(solution)/shard_map/stack | solution.py:114
  55.7 11.8 %fusion.32 = bf16[1,8192,128]{2,1,0:T(8,128)(2,1)S(1)} fusion(s32[]{:T(128)S(6)} %select_n.144, bf16[8192,128]{1,0:T(8,128)(2,1)S(1)} %neg.23, pred[8192]{0:T(1024)(128)(4,1)S(1)} %iota_compare_fusion.1), kind=kLoop, calls=%fused_computation.50 | loop fusion | flops 5242880 | bytes 4202500 | tf_op jit(solution)/shard_map/stack | solution.py:114
  67.5 0.4 pad_maximum_fusion
  67.9 35.4 %copy.69 = bf16[2,8192,128]{2,0,1:T(2,128)(2,1)} copy(bf16[2,8192,128]{2,1,0:T(8,128)(2,1)S(1)} %pad_maximum_fusion) | data formatting | bytes 8388608 | tf_op jit(solution)/shard_map/stack | solution.py:114
  103.3 6.8 %all-to-all-start.1 = ((bf16[2,8192,128]{2,0,1:T(2,128)(2,1)}), bf16[2,8192,128]{2,0,1:T(2,128)(2,1)}, u32[]{:S(2)}, u32[]{:S(2)}) async-start(bf16[2,8192,128]{2,0,1:T(2,128)(2,1)} %copy.69), calls=%async_computation.1 | async-start | bytes 8388608 | tf_op jit(solution)/shard_map/all_to_all | solution.py:166
  110.2 0.8 fusion.40
  111.0 110.5 %all-reduce = (f32[]{:T(128)}, f32[]{:T(128)}) all-reduce(f32[]{:T(128)} %fusion.40, f32[]{:T(128)} %bitcast.21), channel_id=1, replica_groups=mesh['groups'=2,'band'=8,'sub'=2] {'band','sub'}, use_global_device_ids=true, to_apply=%region_3.4 | all-reduce | flops 2 | bytes 16 | tf_op jit(solution)/shard_map/psum | solution.py:146
  222.9 4.7 %copy.70 = bf16[2,8192,128]{2,1,0:T(8,128)(2,1)} copy(bf16[2,8192,128]{2,0,1:T(2,128)(2,1)} %all-to-all-done.1) | data formatting | bytes 8388608 | tf_op jit(solution)/shard_map/all_to_all | solution.py:166
  227.6 6.4 %copy.71 = bf16[16,2,512,128]{2,3,1,0:T(8,128)(2,1)} copy(bf16[16,2,512,128]{3,2,0,1:T(8,128)(2,1)} %bitcast.69) | data formatting | bytes 8388608 | tf_op jit(solution)/shard_map/all_to_all | solution.py:166
  234.1 23.2 %copy.73 = bf16[32,512,2,2,32]{4,0,3,2,1:T(8,128)(2,1)} copy(bf16[32,512,2,2,32]{1,4,3,2,0:T(8,128)(2,1)} %bitcast.67) | data formatting | bytes 8388608 | tf_op jit(solution)/shard_map/reshape | solution.py:118
  257.3 21.0 %convolution_bitcast_fusion = f32[512,2,32,32]{3,2,1,0:T(8,128)} fusion(bf16[32,512,2,2,32]{4,0,3,2,1:T(8,128)(2,1)} %copy.73), kind=kOutput, calls=%fused_computation.40 | convolution fusion | flops 134217728 | bytes 8388608 | tf_op jit(solution)/shard_map/slerm,slern->lemn/dot_general | solution.py:119
  278.3 11.4 %copy.74 = f32[512,2,32,32]{0,3,2,1:T(8,128)} copy(f32[512,2,32,32]{3,2,1,0:T(8,128)} %convolution_bitcast_fusion) | data formatting | bytes 8388608 | tf_op jit(solution)/shard_map/slerm,slern->lemn/dot_general | solution.py:119
  289.7 5.1 %multiply_divide_fusion = f32[512,2,32,32]{0,3,2,1:T(8,128)} fusion(f32[512,2,32,32]{0,3,2,1:T(8,128)} %copy.74, f32[512]{0:T(512)S(1)} %convert_multiply_fusion), kind=kLoop, calls=%fused_computation.47 | loop fusion | flops 2097152 | bytes 8390656 | tf_op jit(solution)/shard_map/div | solution.py:128
  294.8 7.3 %copy.75 = f32[512,2,1024]{2,1,0:T(2,128)} copy(f32[512,2,1024]{0,2,1:T(8,128)} %bitcast.68) | data formatting | bytes 8388608
  (58 shorter events, 6.1 us)
Async XLA Ops:
  3.0 35.1 %copy-start.2 = (s32[16]{0:T(128)S(1)}, s32[16]{0:T(128)}, u32[]{:S(2)}) copy-start(s32[16]{0:T(128)} %param.12) | copy-start | bytes 196
  3.0 45.5 %copy-start = (bf16[1,8192,32]{1,2,0:T(8,128)(2,1)S(1)}, bf16[1,8192,32]{1,2,0:T(8,128)(2,1)}, u32[]{:S(2)}) copy-start(bf16[1,8192,32]{1,2,0:T(8,128)(2,1)} %param.13) | copy-start | bytes 1572868
  38.9 9.7 %all-to-all-start = ((bf16[16,2,1,128]{3,1,2,0:T(2,128)(2,1)}), bf16[16,2,1,128]{3,1,2,0:T(2,128)(2,1)S(1)}, u32[]{:S(2)}, u32[]{:S(2)}) async-start(bf16[16,2,1,128]{3,1,2,0:T(2,128)(2,1)} %select_convert_fusion.3), calls=%async_computation | async-start | bytes 16384 | tf_op jit(solution)/shard_map/all_to_all | solution.py:154
  103.3 6.8 %copy-start.1 = (f32[16384]{0:T(1024)S(1)}, f32[16384]{0:T(1024)}, u32[]{:S(2)}) copy-start(f32[16384]{0:T(1024)} %get-tuple-element.441) | copy-start | bytes 196612
  103.3 119.5 %all-to-all-start.1 = ((bf16[2,8192,128]{2,0,1:T(2,128)(2,1)}), bf16[2,8192,128]{2,0,1:T(2,128)(2,1)}, u32[]{:S(2)}, u32[]{:S(2)}) async-start(bf16[2,8192,128]{2,0,1:T(2,128)(2,1)} %copy.69), calls=%async_computation.1 | async-start | bytes 8388608 | tf_op jit(solution)/shard_map/all_to_all | solution.py:166
where the time goes:
time: 304 us; the launch traced here: 302 us
  blocking collectives  111 us (37%)
  local copies, waits for them, and re-layouts  95.9 us (32%)
  other arithmetic  45.7 us (15%)
  matrix products  31.5 us (10%)
  starting transfers between devices  12.4 us (4%)
  between operations  5.55 us (2%)
    psum x1, blocking collectives, local(): lax.psum((local_square, local_pixels), ('band', 'sub'))  111 us
    another operation x1, local copies, waits for them, and re-layouts, dense_pair(): return jnp.stack([first_dense, second_dense], axis=0)  35.4 us
    reshape x1, local copies, waits for them, and re-layouts, outer_totals(): split_parts = rows.reshape(rows.shape[0], rows.shape[1], 2, 2, maps_count)  23.2 us
    dot_general x1, matrix products, outer_totals(): jnp.einsum('slerm,slern->lemn', split_parts, split_parts, preferred_eleme...  21 us
    another operation x3, other arithmetic, dense_pair(): return jnp.stack([first_dense, second_dense], axis=0)  17.6 us
    dot_general x1, local copies, waits for them, and re-layouts, outer_totals(): jnp.einsum('slerm,slern->lemn', split_parts, split_parts, preferred_eleme...  11.4 us
    all_to_all x2, local copies, waits for them, and re-layouts, local(): lax.all_to_all(dense_local, ('band', 'sub'), split_axis=1, concat_axis=0,...  11.2 us
    dot_general x8, matrix products, add_block(): lax.dot_general(tables, masked, (((1,), (1,)), ((), ())), preferred_eleme...  9.41 us
  transfers between devices with their start and end apart: 2, of which 0 were waited for; matrix products, arithmetic and copies ran while one was open for 1% of the time, Pallas kernels for 0%

commit v1 on v0

--- a/solution.py
+++ b/solution.py
@@ -163,8 +163,14 @@
     alm_pairs = [pair_alm(legendre[0], first_order, first_block, second_block)]
     alm_packed = jnp.stack(alm_pairs, axis=0)
     dense_local = dense_pair(alm_pairs[0], first_order)
-    by_degree = lax.all_to_all(
-        dense_local, ("band", "sub"), split_axis=1, concat_axis=0, tiled=True
+    by_degree = jnp.concatenate(
+        lax.all_to_all(
+            jnp.stack(jnp.split(dense_local, lax.axis_size(("band", "sub")), axis=1)),
+            ("band", "sub"),
+            0,
+            0,
+        ),
+        axis=0,
     )
     degree_local = by_degree.shape[1]
     degrees = device_index * degree_local + jnp.arange(degree_local, dtype=jnp.int32)

time: 304 us -> 275 us (0.905)
  local copies, waits for them, and re-layouts: 95.9 us -> 55.7 us
  other arithmetic: 45.7 us -> 56.9 us
    reshape x1 -> x0, local copies, waits for them, and re-layouts: 23.2 us -> none  [outer_totals(): split_parts = rows.reshape(rows.shape[0], rows.shape[1], 2, 2, maps_count)]
    another operation x1, local copies, waits for them, and re-layouts: 35.4 us -> 23.2 us  [outer_totals(): split_parts = rows.reshape(rows.shape[0], rows.shape[1], 2, 2, maps_count)]
    unnamed x0 -> x15, other arithmetic: none -> 10.8 us
    all_to_all x2 -> x1, local copies, waits for them, and re-layouts: 11.2 us -> 6.4 us  [local(): lax.all_to_all(jnp.stack(jnp.split(dense_local, lax.axis_size(('band', 's...]
    another operation x3 -> x2, other arithmetic: 17.6 us -> 17.2 us  [dense_pair(): return jnp.stack([first_dense, second_dense], axis=0)]
where the time goes in v1:
time: 275 us; the launch traced here: 273 us
  blocking collectives  111 us (40%)
  other arithmetic  56.9 us (21%)
  local copies, waits for them, and re-layouts  55.7 us (20%)
  matrix products  31.5 us (11%)
  starting transfers between devices  12.4 us (5%)
  between operations  5.55 us (2%)
    psum x1, blocking collectives, local(): lax.psum((local_square, local_pixels), ('band', 'sub'))  111 us
    another operation x1, local copies, waits for them, and re-layouts, outer_totals(): split_parts = rows.reshape(rows.shape[0], rows.shape[1], 2, 2, maps_count)  23.2 us
    dot_general x1, matrix products, outer_totals(): jnp.einsum('slerm,slern->lemn', split_parts, split_parts, preferred_eleme...  21 us
    another operation x2, other arithmetic, dense_pair(): return jnp.stack([first_dense, second_dense], axis=0)  17.2 us
    dot_general x1, local copies, waits for them, and re-layouts, outer_totals(): jnp.einsum('slerm,slern->lemn', split_parts, split_parts, preferred_eleme...  11.4 us
    unnamed x15, other arithmetic  10.8 us
    dot_general x8, matrix products, add_block(): lax.dot_general(tables, masked, (((1,), (1,)), ((), ())), preferred_eleme...  9.41 us
    unnamed x10, local copies, waits for them, and re-layouts  7.43 us
  transfers between devices with their start and end apart: 2, of which 0 were waited for; matrix products, arithmetic and copies ran while one was open for 1% of the time, Pallas kernels for 0%

profile of v1, /device:TPU:18, one launch (start us, length us, event | category | flops | bytes accessed | tf_op | source)
XLA Modules:
  0.0 273.0 jit_solution(2661794675630945643)
XLA Ops:
  1.4 0.7 subtract_bitcast_fusion
  2.0 0.7 pad_add_fusion
  3.1 34.6 %while.14 = (s32[]{:T(128)}, f32[64,64]{1,0:T(8,128)S(1)}, s32[]{:T(128)}, f32[]{:T(128)}, s32[32]{0:T(128)S(1)}, /*index=5*/s32[]{:T(128)}, s32[]{:T(128)}, pre...) while((s32[]{:T(128)}, f32[64,64]{1,0:T(8,128)S(1)}, ...), condition=%wide.region_1.2_spmd.clone.clone, body=%wide.region_0.1_spmd.clone.clone.sunk | while | flops 18404532 | bytes 1446522 | solution.py:62
  3.4 0.8 and_select_fusion.4
  4.8 0.7 dynamic_slice.63
  5.5 0.7 add_compare_fusion.3
  6.2 1.2 convolution_add_fusion.2
  7.8 0.8 and_select_fusion.4
  9.2 0.7 dynamic_slice.63
  9.9 0.7 add_compare_fusion.3
  10.5 1.2 convolution_add_fusion.2
  12.1 0.8 and_select_fusion.4
  13.5 0.7 dynamic_slice.63
  14.2 0.7 add_compare_fusion.3
  14.9 1.2 convolution_add_fusion.2
  16.4 0.8 and_select_fusion.4
  17.8 0.7 dynamic_slice.63
  19.2 1.2 convolution_add_fusion.2
  20.8 0.8 and_select_fusion.4
  22.2 0.7 dynamic_slice.63
  22.9 0.7 add_compare_fusion.3
  23.5 1.2 convolution_add_fusion.2
  25.1 0.8 and_select_fusion.4
  26.5 0.7 dynamic_slice.63
  27.2 0.7 add_compare_fusion.3
  27.9 1.2 convolution_add_fusion.2
  29.4 0.8 and_select_fusion.4
  30.8 0.7 dynamic_slice.63
  32.2 1.2 convolution_add_fusion.2
  33.7 0.8 and_select_fusion.4
  35.2 0.7 dynamic_slice.63
  35.9 0.7 add_compare_fusion.3
  36.5 1.2 convolution_add_fusion.2
  38.3 0.7 select_convert_fusion.3
  38.9 5.6 %all-to-all-start = ((bf16[16,2,1,128]{3,1,2,0:T(2,128)(2,1)}), bf16[16,2,1,128]{3,1,2,0:T(2,128)(2,1)S(1)}, u32[]{:S(2)}, u32[]{:S(2)}) async-start(bf16[16,2,1,128]{3,1,2,0:T(2,128)(2,1)} %select_convert_fusion.3), calls=%async_computation | async-start | bytes 16384 | tf_op jit(solution)/shard_map/all_to_all | solution.py:154
  45.8 0.7 iota_compare_fusion.1
  49.0 0.9 fusion.34
  50.3 5.4 %fusion.31 = (bf16[1,8192,128]{2,1,0:T(8,128)(2,1)S(1)}, f32[1,8192,128]{2,1,0:T(8,128)}) fusion(pred[8192]{0:T(1024)(128)(4,1)S(1)} %iota_compare_fusion, f32[8192,128]{1,0:T(8,128)S(1)} %fusion.33), kind=kLoop, calls=%fused_computation.78 | loop fusion | flops 3145728 | bytes 10493952 | tf_op jit(solution)/shard_map/stack | solution.py:114
  55.7 11.8 %fusion.32 = bf16[1,8192,128]{2,1,0:T(8,128)(2,1)S(1)} fusion(s32[]{:T(128)S(6)} %select_n.144, bf16[8192,128]{1,0:T(8,128)(2,1)S(1)} %neg.23, pred[8192]{0:T(1024)(128)(4,1)S(1)} %iota_compare_fusion.1), kind=kLoop, calls=%fused_computation.79 | loop fusion | flops 5242880 | bytes 4202500 | tf_op jit(solution)/shard_map/stack | solution.py:114
  67.5 0.7 bitcast_dynamic-update-slice_fusion.14
  68.2 0.7 bitcast_dynamic-update-slice_fusion.13
  69.0 0.7 bitcast_dynamic-update-slice_fusion.12
  69.7 0.7 bitcast_dynamic-update-slice_fusion.11
  70.4 0.7 bitcast_dynamic-update-slice_fusion.10
  71.1 0.7 bitcast_dynamic-update-slice_fusion.9
  71.8 0.7 bitcast_dynamic-update-slice_fusion.8
  72.6 0.7 bitcast_dynamic-update-slice_fusion.7
  73.3 0.7 bitcast_dynamic-update-slice_fusion.6
  74.0 0.7 bitcast_dynamic-update-slice_fusion.5
  74.7 0.7 bitcast_dynamic-update-slice_fusion.4
  75.4 0.7 bitcast_dynamic-update-slice_fusion.3
  76.2 0.7 bitcast_dynamic-update-slice_fusion.2
  76.9 0.7 bitcast_dynamic-update-slice_fusion.1
  77.6 0.7 bitcast_dynamic-update-slice_fusion
  78.3 0.7 fusion.54
  79.0 6.8 %all-to-all-start.1 = ((bf16[16,2,512,128]{3,2,1,0:T(8,128)(2,1)}), bf16[16,2,512,128]{3,2,1,0:T(8,128)(2,1)}, u32[]{:S(2)}, u32[]{:S(2)}) async-start(bf16[16,2,512,128]{3,2,1,0:T(8,128)(2,1)} %fusion.54), calls=%async_computation.1 | async-start | bytes 8388608 | tf_op jit(solution)/shard_map/all_to_all | solution.py:167
  85.9 0.8 fusion.57
  86.7 110.5 %all-reduce = (f32[]{:T(128)}, f32[]{:T(128)}) all-reduce(f32[]{:T(128)} %fusion.57, f32[]{:T(128)} %bitcast.35), channel_id=1, replica_groups=mesh['groups'=2,'band'=8,'sub'=2] {'band','sub'}, use_global_device_ids=true, to_apply=%region_3.4 | all-reduce | flops 2 | bytes 16 | tf_op jit(solution)/shard_map/psum | solution.py:146
  198.6 6.4 %copy.64 = bf16[16,2,512,128]{2,3,1,0:T(8,128)(2,1)} copy(bf16[16,2,512,128]{3,2,1,0:T(8,128)(2,1)} %all-to-all-done.1) | data formatting | bytes 8388608 | tf_op jit(solution)/shard_map/all_to_all | solution.py:167
  205.0 23.2 %copy.66 = bf16[32,512,2,2,32]{4,0,3,2,1:T(8,128)(2,1)} copy(bf16[32,512,2,2,32]{1,4,3,2,0:T(8,128)(2,1)} %bitcast.98) | data formatting | bytes 8388608 | tf_op jit(solution)/shard_map/reshape;reshape | solution.py:118
  228.2 21.0 %convolution_bitcast_fusion = f32[512,2,32,32]{3,2,1,0:T(8,128)} fusion(bf16[32,512,2,2,32]{4,0,3,2,1:T(8,128)(2,1)} %copy.66), kind=kOutput, calls=%fused_computation.70 | convolution fusion | flops 134217728 | bytes 8388608 | tf_op jit(solution)/shard_map/slerm,slern->lemn/dot_general | solution.py:119
  249.3 11.4 %copy.67 = f32[512,2,32,32]{0,3,2,1:T(8,128)} copy(f32[512,2,32,32]{3,2,1,0:T(8,128)} %convolution_bitcast_fusion) | data formatting | bytes 8388608 | tf_op jit(solution)/shard_map/slerm,slern->lemn/dot_general | solution.py:119
  260.7 5.1 %multiply_divide_fusion = f32[512,2,32,32]{0,3,2,1:T(8,128)} fusion(f32[512,2,32,32]{0,3,2,1:T(8,128)} %copy.67, f32[512]{0:T(512)S(1)} %convert_multiply_fusion), kind=kLoop, calls=%fused_computation.76 | loop fusion | flops 2097152 | bytes 8390656 | tf_op jit(solution)/shard_map/div | solution.py:128
  265.7 7.3 %copy.68 = f32[512,2,1024]{2,1,0:T(2,128)} copy(f32[512,2,1024]{0,2,1:T(8,128)} %bitcast.99) | data formatting | bytes 8388608
  (71 shorter events, 11.5 us)
Async XLA Ops:
  3.0 35.1 %copy-start.2 = (s32[16]{0:T(128)S(1)}, s32[16]{0:T(128)}, u32[]{:S(2)}) copy-start(s32[16]{0:T(128)} %param.12) | copy-start | bytes 196
  3.0 45.5 %copy-start = (bf16[1,8192,32]{1,2,0:T(8,128)(2,1)S(1)}, bf16[1,8192,32]{1,2,0:T(8,128)(2,1)}, u32[]{:S(2)}) copy-start(bf16[1,8192,32]{1,2,0:T(8,128)(2,1)} %param.13) | copy-start | bytes 1572868
  38.9 9.7 %all-to-all-start = ((bf16[16,2,1,128]{3,1,2,0:T(2,128)(2,1)}), bf16[16,2,1,128]{3,1,2,0:T(2,128)(2,1)S(1)}, u32[]{:S(2)}, u32[]{:S(2)}) async-start(bf16[16,2,1,128]{3,1,2,0:T(2,128)(2,1)} %select_convert_fusion.3), calls=%async_computation | async-start | bytes 16384 | tf_op jit(solution)/shard_map/all_to_all | solution.py:154
  79.0 6.8 %copy-start.1 = (f32[16384]{0:T(1024)S(1)}, f32[16384]{0:T(1024)}, u32[]{:S(2)}) copy-start(f32[16384]{0:T(1024)} %get-tuple-element.439) | copy-start | bytes 196612
  79.0 119.5 %all-to-all-start.1 = ((bf16[16,2,512,128]{3,2,1,0:T(8,128)(2,1)}), bf16[16,2,512,128]{3,2,1,0:T(8,128)(2,1)}, u32[]{:S(2)}, u32[]{:S(2)}) async-start(bf16[16,2,512,128]{3,2,1,0:T(8,128)(2,1)} %fusion.54), calls=%async_computation.1 | async-start | bytes 8388608 | tf_op jit(solution)/shard_map/all_to_all | solution.py:167
